TPU v7x, 32 devices: a whole 2x2x4 slice. The times are simulated.
32 devices in a mesh: parts: 2 (over y), expert: 8 (over z, x), dp: 2 (over core).
Axes of the slice: x: 2, y: 2, z: 4, core: 2. Of those that a mesh axis runs over, the one named last changes fastest.
Arguments:
- tokens: bfloat16 [4096, 2048], P(('parts', 'expert', 'dp')), parts along dimension 0, may hold values from -6 to 6
- route_ids: int32 [4096, 2], P(('parts', 'expert', 'dp')), parts along dimension 0, may hold values from 0 to 31, all different within a row; in each aligned block of 128 rows (0 to 127, 128 to 255, ...) at most 10 rows name the same one
- route_gates: float32 [4096, 2], P(('parts', 'expert', 'dp')), parts along dimension 0, may hold values from 0.1 to 1
- gate_weight: bfloat16 [32, 2048, 1408], P('expert', None, 'dp'), may hold values from -0.125 to 0.125
- up_weight: bfloat16 [32, 2048, 1408], P('expert', None, 'dp'), may hold values from -0.125 to 0.125
- down_weight: bfloat16 [32, 1408, 2048], P('expert'), may hold values from -0.15625 to 0.15625
Outputs:
- output: bfloat16 [4096, 2048], P(('parts', 'expert', 'dp')), parts along dimension 0
There are 2 independent parts, one for each index of `parts`. A program takes and returns all parts, laid end to end along the dimension named above; an argument that names none is the same for every part. Nothing has to cross between parts.
Inputs may be any that keep to these rules, and one draw needn't show every extreme that they name: `route_ids`: each row names 2 different experts; within the rows of one device (aligned blocks of 128 rows) no expert is named by more than 10 rows, a bound that some block reaches.
All inputs are finite; a program needn't handle non-finite values.
Results may differ from a plain program's by a relative error of at most 0.0058.
Values may be sent and summed in bfloat16 or wider, within the bound.
No kernel may reach another device: no remote copies, remote signals or barrier semaphores. Data moves between devices by JAX's collectives and lax.ppermute only.
A program may use at most 192 MiB of HBM per device.

v0:
```python
import jax
import jax.numpy as jnp
from jax import lax
from jax.sharding import PartitionSpec as P

FF = 1408
EXPERTS = 32
CAP = 10


def on_device(tokens, route_ids, route_gates, gate_weight, up_weight, down_weight):
    row_count = tokens.shape[0]
    width = tokens.shape[1]
    local_segs = gate_weight.shape[0]
    seg_width = down_weight.shape[1]
    groups = lax.axis_size("expert")
    per_expert = FF // seg_width
    expert_iota = jnp.arange(EXPERTS, dtype=jnp.int32)
    matched = route_ids[:, :, None] == expert_iota[None, None, :]
    member = jnp.sum(matched.astype(jnp.int32), axis=1)
    weighting = jnp.sum(jnp.where(matched, route_gates[:, :, None], jnp.float32(0.0)), axis=1)
    ranking = jnp.cumsum(member, axis=0) - member
    slot_iota = jnp.arange(CAP, dtype=jnp.int32)
    placed = (member[:, :, None] == 1) & (ranking[:, :, None] == slot_iota[None, None, :])
    placed_flat = placed.reshape(row_count, EXPERTS * CAP)
    chooser = placed_flat.astype(jnp.bfloat16)
    packed = jnp.dot(chooser.T, tokens, preferred_element_type=jnp.float32).astype(jnp.bfloat16)
    packed_four = packed.reshape(EXPERTS, 1, CAP, width)
    outgoing = jnp.broadcast_to(packed_four, (EXPERTS, per_expert, CAP, width))
    outgoing = outgoing.reshape(groups, local_segs, CAP, width)
    incoming = lax.all_to_all(outgoing, "expert", split_axis=0, concat_axis=0, tiled=True)
    full_gate, full_up = (
        lax.all_gather(gate_weight, "dp", axis=2, tiled=True),
        lax.all_gather(up_weight, "dp", axis=2, tiled=True),
    )
    gate_val = jnp.einsum("gscd,sdf->gscf", incoming, full_gate, preferred_element_type=jnp.float32)
    up_val = jnp.einsum("gscd,sdf->gscf", incoming, full_up, preferred_element_type=jnp.float32)
    hidden = (jax.nn.silu(gate_val) * up_val).astype(jnp.bfloat16)
    partial_value = jnp.einsum(
        "gscf,sfd->gscd", hidden, down_weight, preferred_element_type=jnp.float32
    ).astype(jnp.bfloat16)
    returned = lax.all_to_all(partial_value, "expert", split_axis=0, concat_axis=0, tiled=True)
    per_seg = returned.reshape(EXPERTS, per_expert, CAP, width).astype(jnp.float32)
    expert_out = jnp.sum(per_seg, axis=1).reshape(EXPERTS * CAP, width)
    combine = jnp.where(placed, weighting[:, :, None], jnp.float32(0.0)).reshape(
        row_count, EXPERTS * CAP
    )
    output = jnp.dot(
        combine, expert_out, precision=lax.Precision.HIGHEST, preferred_element_type=jnp.float32
    )
    return output.astype(jnp.bfloat16)


def solution(mesh):
    placed = (
        P(("parts", "expert", "dp"), None),
        P(("parts", "expert", "dp"), None),
        P(("parts", "expert", "dp"), None),
        P("expert", None, "dp"),
        P("expert", None, "dp"),
        P("expert", None, None),
    )
    return jax.shard_map(
        on_device,
        mesh=mesh,
        in_specs=placed,
        out_specs=P(("parts", "expert", "dp"), None),
        check_vma=False,
    )
```

profile of v0, /device:TPU:0, one launch (start us, length us, event | category | flops | bytes accessed | tf_op | source)
XLA Modules:
  0.0 167.0 jit_solution(10947640230947168460)
XLA Ops:
  6.5 0.0 copy-start
  6.5 0.0 all-gather.3.cloned.1.call-start
  6.5 0.7 all-gather.3.cloned.1.call-update
  7.3 0.0 copy-start.2
  7.3 0.0 all-gather.5.cloned.1.call-start
  7.3 0.7 all-gather.5.cloned.1.call-update
  8.0 0.0 copy-done.2
  8.0 0.1 copy.25
  8.1 0.2 reduce_window_sum.11
  8.3 0.1 copy.27
  8.6 0.1 eq.66
  8.7 0.0 copy-done
  8.7 1.6 convolution_convert_fusion
  10.3 2.3 %reshape_reshape.3 = bf16[8,4,10,2048]{3,2,1,0:T(8,128)(2,1)S(1)} reshape(bf16[320,2048]{1,0:T(8,128)(2,1)} %convolution_convert_fusion) | data formatting | bytes 2621440 | tf_op jit(solution)/shard_map/reshape;reshape | solution.py:30
  12.6 1.0 copy.28
  13.6 38.4 %all_to_all.10 = bf16[8,4,10,2048]{3,1,2,0:T(4,128)(2,1)S(1)} all-to-all(bf16[8,4,10,2048]{3,1,2,0:T(4,128)(2,1)S(1)} %copy.28), channel_id=1, replica_groups=mesh['parts'=2,'expert'=8,'dp'=2] {'expert'}, dimensions={0} | all-to-all | bytes 2621440 | tf_op jit(solution)/shard_map/all_to_all | solution.py:31
  52.1 0.0 all-gather.3.cloned.1.call-done
  52.1 15.3 %fusion.6 = f32[8,4,10,1408]{3,2,0,1:T(8,128)} fusion(bf16[4,2048,1408]{1,2,0:T(8,128)(2,1)} %all-gather.3.cloned.1.call-done, bf16[8,4,10,2048]{3,1,2,0:T(4,128)(2,1)S(1)} %all_to_all.10), kind=kOutput, calls=%fused_computation.6 | convolution fusion | flops 1845493760 | bytes 26181632 | tf_op jit(solution)/shard_map/gscd,sdf->gscf/dot_general | solution.py:36
  67.3 22.3 %all-gather.5.cloned.1.call-done = bf16[4,2048,1408]{1,2,0:T(8,128)(2,1)} async-done(((bf16[4,2048,704]{1,2,0:T(8,128)(2,1)}), bf16[4,2048,1408]{1,2,0:T(8,128)(2,1)}) %all-gather.5.cloned.1.call-update) | async-done | bytes 23068688 | tf_op jit(solution)/shard_map/all_gather | solution.py:34
  89.6 12.9 %fusion.15 = bf16[8,4,10,1408]{3,2,0,1:T(8,128)(2,1)S(1)} fusion(bf16[4,2048,1408]{1,2,0:T(8,128)(2,1)} %all-gather.5.cloned.1.call-done, f32[8,4,10,1408]{3,2,0,1:T(8,128)} %fusion.6, bf16[8,4,10,2048]{3,1,2,0:T(4,128)(2,1)S(1)} %all_to_all.10), kind=kOutput, calls=%fused_computation.9 | convolution fusion | flops 1848197120 | bytes 27082752 | tf_op jit(solution)/shard_map/gscd,sdf->gscf/dot_general | solution.py:37
  102.6 11.0 %fusion.21 = bf16[8,4,10,2048]{3,2,0,1:T(8,128)(2,1)S(1)} fusion(bf16[8,4,10,1408]{3,2,0,1:T(8,128)(2,1)S(1)} %fusion.15, bf16[4,1408,2048]{2,1,0:T(8,128)(2,1)} %param.11), kind=kOutput, calls=%fused_computation.11 | convolution fusion | flops 1846149120 | bytes 25280512 | tf_op jit(solution)/shard_map/gscf,sfd->gscd/dot_general | solution.py:39
  113.6 0.0 copy-start.3
  113.6 2.1 %copy.31 = bf16[8,4,10,2048]{3,1,2,0:T(4,128)(2,1)} copy(bf16[8,4,10,2048]{3,2,0,1:T(8,128)(2,1)S(1)} %fusion.21) | data formatting | bytes 2621440 | tf_op jit(solution)/shard_map/convert_element_type | solution.py:41
  115.7 5.8 %all-to-all-start.1 = ((bf16[8,4,10,2048]{3,1,2,0:T(4,128)(2,1)}), bf16[8,4,10,2048]{3,1,2,0:T(4,128)(2,1)}, u32[]{:S(2)}, u32[]{:S(2)}) async-start(bf16[8,4,10,2048]{3,1,2,0:T(4,128)(2,1)} %copy.31), calls=%async_computation.1 | async-start | bytes 2621440 | tf_op jit(solution)/shard_map/all_to_all | solution.py:42
  121.5 0.0 copy-done.3
  121.5 0.1 fusion.27
  121.6 31.8 %all-to-all-done.1 = bf16[8,4,10,2048]{3,1,2,0:T(4,128)(2,1)} async-done(((bf16[8,4,10,2048]{3,1,2,0:T(4,128)(2,1)}), bf16[8,4,10,2048]{3,1,2,0:T(4,128)(2,1)}, u32[]{:S(2)}, u32[]{:S(2)}) %all-to-all-start.1) | async-done | bytes 1310752 | tf_op jit(solution)/shard_map/all_to_all | solution.py:42
  153.4 0.0 copy-start.1
  153.4 2.3 %copy.32 = bf16[8,4,10,2048]{3,2,1,0:T(8,128)(2,1)S(1)} copy(bf16[8,4,10,2048]{3,1,2,0:T(4,128)(2,1)} %all-to-all-done.1) | data formatting | bytes 2621440 | tf_op jit(solution)/shard_map/all_to_all | solution.py:42
  155.7 1.3 reshape.68
  157.0 3.1 %convolution_convert_fusion.1 = bf16[128,2048]{1,0:T(8,128)(2,1)} fusion(f32[128,320]{0,1:T(8,128)S(1)} %select_n.20, bf16[320,2048]{1,0:T(8,128)(2,1)} %reshape.68), kind=kOutput, calls=%fused_computation.13 | convolution fusion | flops 1006895104 | bytes 1998848 | tf_op jit(solution)/shard_map/dot_general | solution.py:48
  160.1 0.0 copy-done.1
  (10 shorter events, 0.2 us)
Async XLA Ops:
  6.5 2.1 %copy-start = (bf16[128,2048]{1,0:T(8,128)(2,1)S(1)}, bf16[128,2048]{1,0:T(8,128)(2,1)}, u32[]{:S(2)}) copy-start(bf16[128,2048]{1,0:T(8,128)(2,1)} %param.6) | copy-start | bytes 1572868
  6.5 45.6 %all-gather.3.cloned.1.call-start = ((), (), s32[]{:S(2)}) async-start(), calls=%async_computation.2 | async-start | bytes 34603008 | tf_op jit(solution)/shard_map/all_gather | solution.py:33
  7.3 0.8 copy-start.2
  7.3 82.4 %all-gather.5.cloned.1.call-start = ((), (), s32[]{:S(2)}) async-start(), calls=%async_computation.3 | async-start | bytes 34603008 | tf_op jit(solution)/shard_map/all_gather | solution.py:34
  113.6 7.9 %copy-start.3 = (f32[128,2]{0,1:T(2,128)S(1)}, f32[128,2]{0,1:T(2,128)}, u32[]{:S(2)}) copy-start(f32[128,2]{0,1:T(2,128)} %param.8) | copy-start | bytes 3076
  115.7 37.7 %all-to-all-start.1 = ((bf16[8,4,10,2048]{3,1,2,0:T(4,128)(2,1)}), bf16[8,4,10,2048]{3,1,2,0:T(4,128)(2,1)}, u32[]{:S(2)}, u32[]{:S(2)}) async-start(bf16[8,4,10,2048]{3,1,2,0:T(4,128)(2,1)} %copy.31), calls=%async_computation.1 | async-start | bytes 2621440 | tf_op jit(solution)/shard_map/all_to_all | solution.py:42
  153.4 6.7 %copy-start.1 = (bf16[128,2048]{1,0:T(8,128)(2,1)S(1)}, bf16[128,2048]{1,0:T(8,128)(2,1)}, u32[]{:S(2)}) copy-start(bf16[128,2048]{1,0:T(8,128)(2,1)} %param.6) | copy-start | bytes 1572868
Sparse Core Ops, SparseCore 0:
  8.9 40.3 all-gather.2
  50.8 38.7 all-gather.4
where the time goes:
time: 167 us
  waiting for transfers between devices  55.5 us (33%)
  matrix products  43.9 us (26%)
  blocking collectives  38.4 us (23%)
  between operations  13.6 us (8%)
  local copies, waits for them, and re-layouts  9.43 us (6%)
  starting transfers between devices  5.81 us (3%)
    all_to_all x1, blocking collectives, on_device(): lax.all_to_all(outgoing, 'expert', split_axis=0, concat_axis=0, tiled=True)  38.4 us
    all_to_all x1, waiting for transfers between devices, on_device(): lax.all_to_all(partial_value, 'expert', split_axis=0, concat_axis=0, tile...  31.8 us
    all_gather x1, waiting for transfers between devices, on_device(): lax.all_gather(up_weight, 'dp', axis=2, tiled=True)  22.3 us
    dot_general x1, matrix products, on_device(): jnp.einsum('gscd,sdf->gscf', incoming, full_gate, preferred_element_type=...  15.3 us
    dot_general x1, matrix products, on_device(): jnp.einsum('gscd,sdf->gscf', incoming, full_up, preferred_element_type=jn...  12.9 us
    dot_general x1, matrix products, on_device(): jnp.einsum('gscf,sfd->gscd', hidden, down_weight, preferred_element_type=...  11 us
    all_to_all x1, starting transfers between devices, on_device(): lax.all_to_all(partial_value, 'expert', split_axis=0, concat_axis=0, tile...  5.77 us
  transfers between devices with their start and end apart: 3, of which 2 were waited for; matrix products, arithmetic and copies ran while one was open for 13% of the time, Pallas kernels for 0%

commit v1 on v0

--- a/solution.py
+++ b/solution.py
@@ -6,6 +6,22 @@
 FF = 1408
 EXPERTS = 32
 CAP = 10
+
+
+def pairwise_exchange(x, axis, split, join):
+    ways, here = (lax.axis_size(axis), lax.axis_index(axis))
+    width = x.shape[split] // ways
+    shape = list(x.shape)
+    shape[split] = width
+    height = shape[join]
+    shape[join] = height * ways
+    full = jnp.zeros(shape, x.dtype)
+    for mask in range(ways):
+        part = lax.dynamic_slice_in_dim(x, (here ^ mask) * width, width, axis=split)
+        if mask:
+            part = lax.ppermute(part, axis, [(d, d ^ mask) for d in range(ways)])
+        full = lax.dynamic_update_slice_in_dim(full, part, (here ^ mask) * height, axis=join)
+    return full
 
 
 def on_device(tokens, route_ids, route_gates, gate_weight, up_weight, down_weight):
@@ -39,7 +55,7 @@
     partial_value = jnp.einsum(
         "gscf,sfd->gscd", hidden, down_weight, preferred_element_type=jnp.float32
     ).astype(jnp.bfloat16)
-    returned = lax.all_to_all(partial_value, "expert", split_axis=0, concat_axis=0, tiled=True)
+    returned = pairwise_exchange(partial_value, "expert", 0, 0)
     per_seg = returned.reshape(EXPERTS, per_expert, CAP, width).astype(jnp.float32)
     expert_out = jnp.sum(per_seg, axis=1).reshape(EXPERTS * CAP, width)
     combine = jnp.where(placed, weighting[:, :, None], jnp.float32(0.0)).reshape(

time: 167 us -> 176 us (1.054)
  the two profiles are of different devices: /device:TPU:0 before, /device:TPU:16 now
where the time goes in v1:
time: 176 us
  waiting for transfers between devices  97.7 us (56%)
  matrix products  43.3 us (25%)
  starting transfers between devices  14.5 us (8%)
  between operations  13.6 us (8%)
  local copies, waits for them, and re-layouts  6.8 us (4%)
    ppermute x7, waiting for transfers between devices, pairwise_exchange(): part = lax.ppermute(part, axis, [(d, d ^ mask) for d in range(ways)])  43.8 us
    all_to_all x1, waiting for transfers between devices, on_device(): lax.all_to_all(outgoing, 'expert', split_axis=0, concat_axis=0, tiled=True)  28 us
    all_gather x1, waiting for transfers between devices, on_device(): lax.all_gather(up_weight, 'dp', axis=2, tiled=True)  24.5 us
    dot_general x1, matrix products, on_device(): jnp.einsum('gscd,sdf->gscf', incoming, full_gate, preferred_element_type=...  14.6 us
    dot_general x1, matrix products, on_device(): jnp.einsum('gscd,sdf->gscf', incoming, full_up, preferred_element_type=jn...  12.9 us
    dot_general x1, matrix products, on_device(): jnp.einsum('gscf,sfd->gscd', hidden, down_weight, preferred_element_type=...  11 us
    ppermute x7, starting transfers between devices, pairwise_exchange(): part = lax.ppermute(part, axis, [(d, d ^ mask) for d in range(ways)])  8.14 us
    all_to_all x1, starting transfers between devices, on_device(): lax.all_to_all(outgoing, 'expert', split_axis=0, concat_axis=0, tiled=True)  6.27 us
  transfers between devices with their start and end apart: 10, of which 8 were waited for; matrix products, arithmetic and copies ran while one was open for 12% of the time, Pallas kernels for 0%

profile of v1, /device:TPU:16, one launch (start us, length us, event | category | flops | bytes accessed | tf_op | source)
XLA Modules:
  0.0 176.2 jit_solution(11448239106916631537)
XLA Ops:
  6.5 0.7 all-gather.3.cloned.1.call-update
  7.3 0.7 all-gather.5.cloned.1.call-update
  8.0 0.1 copy.22
  8.1 0.2 reduce_window_sum.11
  8.6 0.1 eq.66
  8.7 1.6 convolution_convert_fusion
  10.3 2.3 %reshape_reshape.3 = bf16[8,4,10,2048]{3,2,1,0:T(8,128)(2,1)S(1)} reshape(bf16[320,2048]{1,0:T(8,128)(2,1)} %convolution_convert_fusion) | data formatting | bytes 2621440 | tf_op jit(solution)/shard_map/reshape;reshape | solution.py:46
  12.6 2.1 %copy.25 = bf16[8,4,10,2048]{3,1,2,0:T(4,128)(2,1)} copy(bf16[8,4,10,2048]{3,2,1,0:T(8,128)(2,1)S(1)} %reshape_reshape.3) | data formatting | bytes 2621440 | tf_op jit(solution)/shard_map/reshape;reshape | solution.py:46
  14.8 6.3 %all-to-all-start = ((bf16[8,4,10,2048]{3,1,2,0:T(4,128)(2,1)}), bf16[8,4,10,2048]{3,1,2,0:T(4,128)(2,1)S(1)}, u32[]{:S(2)}, u32[]{:S(2)}) async-start(bf16[8,4,10,2048]{3,1,2,0:T(4,128)(2,1)} %copy.25), calls=%async_computation | async-start | bytes 2621440 | tf_op jit(solution)/shard_map/all_to_all | solution.py:47
  21.0 0.1 fusion.24
  21.2 28.0 %all-to-all-done = bf16[8,4,10,2048]{3,1,2,0:T(4,128)(2,1)S(1)} async-done(((bf16[8,4,10,2048]{3,1,2,0:T(4,128)(2,1)}), bf16[8,4,10,2048]{3,1,2,0:T(4,128)(2,1)S(1)}, u32[]{:S(2)}, u32[]{:S(2)}) %all-to-all-start) | async-done | bytes 1310752 | tf_op jit(solution)/shard_map/all_to_all | solution.py:47
  49.1 14.6 %fusion.6 = f32[8,4,10,1408]{3,2,0,1:T(8,128)} fusion(bf16[4,2048,1408]{1,2,0:T(8,128)(2,1)} %all-gather.3.cloned.1.call-done, bf16[8,4,10,2048]{3,1,2,0:T(4,128)(2,1)S(1)} %all-to-all-done), kind=kOutput, calls=%fused_computation.6 | convolution fusion | flops 1845493760 | bytes 26181632 | tf_op jit(solution)/shard_map/gscd,sdf->gscf/dot_general | solution.py:52
  63.7 24.5 %all-gather.5.cloned.1.call-done = bf16[4,2048,1408]{1,2,0:T(8,128)(2,1)} async-done(((bf16[4,2048,704]{1,2,0:T(8,128)(2,1)}), bf16[4,2048,1408]{1,2,0:T(8,128)(2,1)}) %all-gather.5.cloned.1.call-update) | async-done | bytes 23068688 | tf_op jit(solution)/shard_map/all_gather | solution.py:50
  88.3 12.9 %fusion.15 = bf16[8,4,10,1408]{3,2,0,1:T(8,128)(2,1)S(1)} fusion(bf16[4,2048,1408]{1,2,0:T(8,128)(2,1)} %all-gather.5.cloned.1.call-done, f32[8,4,10,1408]{3,2,0,1:T(8,128)} %fusion.6, bf16[8,4,10,2048]{3,1,2,0:T(4,128)(2,1)S(1)} %all-to-all-done), kind=kOutput, calls=%fused_computation.9 | convolution fusion | flops 1848197120 | bytes 27082752 | tf_op jit(solution)/shard_map/gscd,sdf->gscf/dot_general | solution.py:53
  101.2 11.0 %fusion.18 = bf16[4,8,10,2048]{3,2,1,0:T(8,128)(2,1)S(1)} fusion(bf16[8,4,10,1408]{3,2,0,1:T(8,128)(2,1)S(1)} %fusion.15, bf16[4,1408,2048]{2,1,0:T(8,128)(2,1)} %param.11), kind=kOutput, calls=%fused_computation.10 | convolution fusion | flops 1846149120 | bytes 25280512 | tf_op jit(solution)/shard_map/gscf,sfd->gscd/dot_general | solution.py:55
  112.2 0.2 dynamic-slice_bitcast_fusion
  112.4 1.5 collective-permute-start
  114.0 1.5 collective-permute-start.1
  115.5 0.5 collective-permute-start.2
  116.0 0.3 collective-permute-start.3
  116.2 3.6 %collective-permute-start.4 = (bf16[1,4,10,2048]{3,2,1,0:T(8,128)(2,1)S(1)}, bf16[1,4,10,2048]{3,2,1,0:T(8,128)(2,1)S(1)}, u32[]{:S(2)}, u32[]{:S(2)}) collective-permute-start(bf16[1,4,10,2048]{3,2,1,0:T(8,128)(2,1)S(1)} %get-tuple-element.7), channel_id=1, source_target_pairs={{0,10},{2,8},{4,14},{6,12},{8,2},{10,0},{12,6},{14,4},{1,11},{3,9}... | collective-permute-start | bytes 491528 | tf_op jit(solution)/shard_map/ppermute | solution.py:22
  119.8 0.2 broadcast_in_dim.38
  120.1 0.9 collective-permute-done
  121.0 0.5 collective-permute-start.5
  121.6 9.5 %collective-permute-done.1 = bf16[1,4,10,2048]{3,2,1,0:T(8,128)(2,1)S(1)} collective-permute-done((bf16[1,4,10,2048]{3,2,1,0:T(8,128)(2,1)S(1)}, bf16[1,4,10,2048]{3,2,1,0:T(8,128)(2,1)S(1)}, u32[]{:S(2)}, u32[]{:S(2)}) %collective-permute-start.1) | collective-permute-done | bytes 163872 | tf_op jit(solution)/shard_map/ppermute | solution.py:22
  131.0 0.2 collective-permute-start.6
  131.3 4.4 %collective-permute-done.2 = bf16[1,4,10,2048]{3,2,1,0:T(8,128)(2,1)S(1)} collective-permute-done((bf16[1,4,10,2048]{3,2,1,0:T(8,128)(2,1)S(1)}, bf16[1,4,10,2048]{3,2,1,0:T(8,128)(2,1)S(1)}, u32[]{:S(2)}, u32[]{:S(2)}) %collective-permute-start.2) | collective-permute-done | bytes 163872 | tf_op jit(solution)/shard_map/ppermute | solution.py:22
  135.8 15.3 %collective-permute-done.4 = bf16[1,4,10,2048]{3,2,1,0:T(8,128)(2,1)S(1)} collective-permute-done((bf16[1,4,10,2048]{3,2,1,0:T(8,128)(2,1)S(1)}, bf16[1,4,10,2048]{3,2,1,0:T(8,128)(2,1)S(1)}, u32[]{:S(2)}, u32[]{:S(2)}) %collective-permute-start.4) | collective-permute-done | bytes 163872 | tf_op jit(solution)/shard_map/ppermute | solution.py:22
  151.1 8.7 %collective-permute-done.5 = bf16[1,4,10,2048]{3,2,1,0:T(8,128)(2,1)S(1)} collective-permute-done((bf16[1,4,10,2048]{3,2,1,0:T(8,128)(2,1)S(1)}, bf16[1,4,10,2048]{3,2,1,0:T(8,128)(2,1)S(1)}, u32[]{:S(2)}, u32[]{:S(2)}) %collective-permute-start.5) | collective-permute-done | bytes 163872 | tf_op jit(solution)/shard_map/ppermute | solution.py:22
  159.9 5.0 %collective-permute-done.6 = bf16[1,4,10,2048]{3,2,1,0:T(8,128)(2,1)S(1)} collective-permute-done((bf16[1,4,10,2048]{3,2,1,0:T(8,128)(2,1)S(1)}, bf16[1,4,10,2048]{3,2,1,0:T(8,128)(2,1)S(1)}, u32[]{:S(2)}, u32[]{:S(2)}) %collective-permute-start.6) | collective-permute-done | bytes 163872 | tf_op jit(solution)/shard_map/ppermute | solution.py:22
  164.9 1.3 reshape.76
  166.2 3.1 %convolution_convert_fusion.1 = bf16[128,2048]{1,0:T(8,128)(2,1)} fusion(f32[128,320]{0,1:T(8,128)S(1)} %select_n.52, bf16[320,2048]{1,0:T(8,128)(2,1)} %reshape.76), kind=kOutput, calls=%fused_computation.12 | convolution fusion | flops 1006895104 | bytes 1998848 | tf_op jit(solution)/shard_map/dot_general | solution.py:64
  (31 shorter events, 0.5 us)
Async XLA Ops:
  6.5 2.1 %copy-start = (bf16[128,2048]{1,0:T(8,128)(2,1)S(1)}, bf16[128,2048]{1,0:T(8,128)(2,1)}, u32[]{:S(2)}) copy-start(bf16[128,2048]{1,0:T(8,128)(2,1)} %param.6) | copy-start | bytes 1572868
  6.5 42.6 %all-gather.3.cloned.1.call-start = ((), (), s32[]{:S(2)}) async-start(), calls=%async_computation.1 | async-start | bytes 34603008 | tf_op jit(solution)/shard_map/all_gather | solution.py:49
  7.3 0.8 copy-start.2
  7.3 81.0 %all-gather.5.cloned.1.call-start = ((), (), s32[]{:S(2)}) async-start(), calls=%async_computation.2 | async-start | bytes 34603008 | tf_op jit(solution)/shard_map/all_gather | solution.py:50
  14.8 6.3 %copy-start.3 = (f32[128,2]{0,1:T(2,128)S(1)}, f32[128,2]{0,1:T(2,128)}, u32[]{:S(2)}) copy-start(f32[128,2]{0,1:T(2,128)} %param.8) | copy-start | bytes 3076
  14.8 34.4 %all-to-all-start = ((bf16[8,4,10,2048]{3,1,2,0:T(4,128)(2,1)}), bf16[8,4,10,2048]{3,1,2,0:T(4,128)(2,1)S(1)}, u32[]{:S(2)}, u32[]{:S(2)}) async-start(bf16[8,4,10,2048]{3,1,2,0:T(4,128)(2,1)} %copy.25), calls=%async_computation | async-start | bytes 2621440 | tf_op jit(solution)/shard_map/all_to_all | solution.py:47
  112.4 8.6 %collective-permute-start = (bf16[1,4,10,2048]{3,2,1,0:T(8,128)(2,1)S(1)}, bf16[1,4,10,2048]{3,2,1,0:T(8,128)(2,1)S(1)}, u32[]{:S(2)}, u32[]{:S(2)}) collective-permute-start(bf16[1,4,10,2048]{3,2,1,0:T(8,128)(2,1)S(1)} %get-tuple-element.11), channel_id=1, source_target_pairs={{0,2},{2,0},{4,6},{6,4},{8,10},{10,8},{12,14},{14,12},{1,3},{3,1},... | collective-permute-start | bytes 491528 | tf_op jit(solution)/shard_map/ppermute | solution.py:22
  114.0 17.1 %collective-permute-start.1 = (bf16[1,4,10,2048]{3,2,1,0:T(8,128)(2,1)S(1)}, bf16[1,4,10,2048]{3,2,1,0:T(8,128)(2,1)S(1)}, u32[]{:S(2)}, u32[]{:S(2)}) collective-permute-start(bf16[1,4,10,2048]{3,2,1,0:T(8,128)(2,1)S(1)} %get-tuple-element.10), channel_id=1, source_target_pairs={{0,4},{2,6},{4,0},{6,2},{8,12},{10,14},{12,8},{14,10},{1,5},{3,7},... | collective-permute-start | bytes 491528 | tf_op jit(solution)/shard_map/ppermute | solution.py:22
  115.5 20.3 %collective-permute-start.2 = (bf16[1,4,10,2048]{3,2,1,0:T(8,128)(2,1)S(1)}, bf16[1,4,10,2048]{3,2,1,0:T(8,128)(2,1)S(1)}, u32[]{:S(2)}, u32[]{:S(2)}) collective-permute-start(bf16[1,4,10,2048]{3,2,1,0:T(8,128)(2,1)S(1)} %get-tuple-element.9), channel_id=1, source_target_pairs={{0,6},{2,4},{4,2},{6,0},{8,14},{10,12},{12,10},{14,8},{1,7},{3,5},... | collective-permute-start | bytes 491528 | tf_op jit(solution)/shard_map/ppermute | solution.py:22
  116.0 19.7 %collective-permute-start.3 = (bf16[1,4,10,2048]{3,2,1,0:T(8,128)(2,1)S(1)}, bf16[1,4,10,2048]{3,2,1,0:T(8,128)(2,1)S(1)}, u32[]{:S(2)}, u32[]{:S(2)}) collective-permute-start(bf16[1,4,10,2048]{3,2,1,0:T(8,128)(2,1)S(1)} %get-tuple-element.8), channel_id=1, source_target_pairs={{0,8},{2,10},{4,12},{6,14},{8,0},{10,2},{12,4},{14,6},{1,9},{3,11}... | collective-permute-start | bytes 491528 | tf_op jit(solution)/shard_map/ppermute | solution.py:22
  116.2 34.8 %collective-permute-start.4 = (bf16[1,4,10,2048]{3,2,1,0:T(8,128)(2,1)S(1)}, bf16[1,4,10,2048]{3,2,1,0:T(8,128)(2,1)S(1)}, u32[]{:S(2)}, u32[]{:S(2)}) collective-permute-start(bf16[1,4,10,2048]{3,2,1,0:T(8,128)(2,1)S(1)} %get-tuple-element.7), channel_id=1, source_target_pairs={{0,10},{2,8},{4,14},{6,12},{8,2},{10,0},{12,6},{14,4},{1,11},{3,9}... | collective-permute-start | bytes 491528 | tf_op jit(solution)/shard_map/ppermute | solution.py:22
  121.0 38.8 %collective-permute-start.5 = (bf16[1,4,10,2048]{3,2,1,0:T(8,128)(2,1)S(1)}, bf16[1,4,10,2048]{3,2,1,0:T(8,128)(2,1)S(1)}, u32[]{:S(2)}, u32[]{:S(2)}) collective-permute-start(bf16[1,4,10,2048]{3,2,1,0:T(8,128)(2,1)S(1)} %get-tuple-element.6), channel_id=1, source_target_pairs={{0,12},{2,14},{4,8},{6,10},{8,4},{10,6},{12,0},{14,2},{1,13},{3,15... | collective-permute-start | bytes 491528 | tf_op jit(solution)/shard_map/ppermute | solution.py:22
  131.0 33.8 %collective-permute-start.6 = (bf16[1,4,10,2048]{3,2,1,0:T(8,128)(2,1)S(1)}, bf16[1,4,10,2048]{3,2,1,0:T(8,128)(2,1)S(1)}, u32[]{:S(2)}, u32[]{:S(2)}) collective-permute-start(bf16[1,4,10,2048]{3,2,1,0:T(8,128)(2,1)S(1)} %get-tuple-element.5), channel_id=1, source_target_pairs={{0,14},{2,12},{4,10},{6,8},{8,6},{10,4},{12,2},{14,0},{1,15},{3,13... | collective-permute-start | bytes 491528 | tf_op jit(solution)/shard_map/ppermute | solution.py:22
  164.9 4.5 %copy-start.1 = (bf16[128,2048]{1,0:T(8,128)(2,1)S(1)}, bf16[128,2048]{1,0:T(8,128)(2,1)}, u32[]{:S(2)}) copy-start(bf16[128,2048]{1,0:T(8,128)(2,1)} %param.6) | copy-start | bytes 1572868
Sparse Core Ops, SparseCore 0:
  8.9 38.9 all-gather.2
  49.4 38.7 all-gather.4
